TPU v7x, 128 devices: a whole 4x4x4 slice. The times are simulated.
128 devices in a mesh: batch: 4 (over z), head: 2 (over core), seq: 16 (over x, y).
Axes of the slice: x: 4, y: 4, z: 4, core: 2. Of those that a mesh axis runs over, the one named last changes fastest.
Arguments:
- hidden: float32 [32768, 8192], P(('batch', 'seq')), parts along dimension 0, may hold values from -6 to 6
- row_scale: float32 [32768], P(('batch', 'seq')), parts along dimension 0, may hold values from 0.25 to 4
- key_value_weight: float32 [8192, 8, 256], P('seq', 'head'), may hold values from -0.0625 to 0.0625
- outlier: int32 [512, 8], P(('batch', 'seq'), 'head'), parts along dimension 0, may hold values 0 or 1
- sketch_sign_flags: int32 [8, 2, 128, 64], P('head'), may hold values from 0 to 1
Outputs:
- left: bfloat16 [8, 32768, 128], P('head', ('batch', 'seq')), parts along dimension 1
- right: float32 [32, 128, 128], P(('batch', 'head')), parts along dimension 0
There are 4 independent parts, one for each index of `batch`. A program takes and returns all parts, laid end to end along the dimension named above; an argument that names none is the same for every part. Nothing has to cross between parts.
All inputs are finite; a program needn't handle non-finite values. No bound on the sum of `outlier` on one device may be relied on, other than what follows from the above.
Results may differ from a plain program's by a relative error of at most 0.0015.
Values sent between devices are 32-bit elements; how exact they have to be, the bound alone decides.
No kernel may reach another device: no remote copies, remote signals or barrier semaphores. Data moves between devices by JAX's collectives and lax.ppermute only.
A program may use at most 192 MiB of HBM per device.

v0:
```python
import math

import jax
import jax.numpy as jnp
from jax import lax
from jax.sharding import PartitionSpec as P

ITERS = 2


complete_cycle = 2.0 * math.pi


def shards(hidden, row_scale, key_value_weight, outlier, sketch_sign_flags):
    tok_rows = hidden.shape[0]
    head_count = key_value_weight.shape[1]
    kv_cols = key_value_weight.shape[2]
    head_dim = kv_cols // 2
    rank_cols = sketch_sign_flags.shape[3]
    group_count = outlier.shape[0]
    highest = lax.Precision.HIGHEST
    weight_piece = lax.all_gather(key_value_weight, "seq", axis=0, tiled=True)
    flat_piece = weight_piece.reshape(weight_piece.shape[0], head_count * kv_cols)
    projected_key_value = jnp.dot(hidden, flat_piece, precision=highest)
    projected_key_value = projected_key_value * row_scale[:, None]
    grouped_rows = projected_key_value.reshape(
        group_count, tok_rows // group_count, head_count, kv_cols
    )
    quantization_spacing = jnp.max(jnp.abs(grouped_rows), axis=1, keepdims=True) / 7.0 + 1e-06
    retain_mask = (1 - outlier).astype(jnp.float32)[:, None, :, None]
    residual_error = (
        retain_mask * jnp.sin(complete_cycle * grouped_rows / quantization_spacing)
    ).reshape(tok_rows, head_count, 2, head_dim)
    sign_matrix = (2 * sketch_sign_flags - 1).astype(jnp.float32)
    sketch = jnp.einsum("thec,heck->thek", residual_error, sign_matrix, precision=highest)
    for iteration in range(ITERS):
        local_gram = jnp.einsum("thek,theq->hekq", sketch, sketch, precision=highest)
        gram_matrix = lax.psum(local_gram, "seq")
        lower_factor = jnp.linalg.cholesky(gram_matrix)
        identity = jnp.broadcast_to(jnp.eye(rank_cols, dtype=gram_matrix.dtype), gram_matrix.shape)
        inverse_factor = jax.scipy.linalg.solve_triangular(lower_factor, identity, lower=True)
        basis_matrix = jnp.einsum("thek,heqk->theq", sketch, inverse_factor, precision=highest)
        local_coef = jnp.einsum("thec,theq->hecq", residual_error, basis_matrix, precision=highest)
        coefficient_rows = lax.psum(local_coef, "seq")
        if iteration + 1 < ITERS:
            sketch = jnp.einsum(
                "thec,hecq->theq", residual_error, coefficient_rows, precision=highest
            )
    root_length = math.sqrt(tok_rows * lax.axis_size("seq"))
    left = (
        (root_length * basis_matrix)
        .transpose(1, 0, 2, 3)
        .reshape(head_count, tok_rows, 2 * rank_cols)
        .astype(jnp.bfloat16)
    )
    right = (
        (coefficient_rows / root_length)
        .transpose(0, 2, 1, 3)
        .reshape(head_count, head_dim, 2 * rank_cols)
    )
    return (left, right)


def solution(mesh):
    return jax.shard_map(
        shards,
        mesh=mesh,
        in_specs=(
            P(("batch", "seq"), None),
            P(("batch", "seq")),
            P("seq", "head", None),
            P(("batch", "seq"), "head"),
            P("head", None, None, None),
        ),
        out_specs=(P("head", ("batch", "seq"), None), P(("batch", "head"), None, None)),
        check_vma=False,
    )
```

profile of v0, /device:TPU:0, one launch (start us, length us, event | category | flops | bytes accessed | tf_op | source)
XLA Modules:
  0.0 858.8 jit_solution(14637617141155702260)
XLA Ops:
  7.2 0.0 copy-start.2
  7.2 0.0 all-gather.2.cloned.1.call-start
  7.2 0.7 all-gather.2.cloned.1.call-update
  7.9 0.0 all-reduce.5.cloned.1.call-start
  8.0 0.0 copy-done.2
  8.0 0.1 mul.45
  8.0 0.1 mul.46
  8.1 201.4 %all-gather.2.cloned.1.call-done = f32[8192,4,256]{2,1,0:T(4,128)} async-done(((f32[512,4,256]{2,1,0:T(4,128)}), f32[8192,4,256]{2,1,0:T(4,128)}) %all-gather.2.cloned.1.call-update) | async-done | bytes 33554448 | tf_op jit(solution)/shard_map/all_gather | solution.py:22
  209.6 0.0 copy-start.3
  209.6 27.5 %copy.108 = f32[1024,8,4,256]{3,1,2,0:T(8,128)} copy(f32[1024,8,4,256]{3,2,1,0:T(4,128)} %bitcast.58) | data formatting | bytes 67108864
  237.1 0.0 copy-done.3
  237.1 60.5 %multiply_abs_fusion = (f32[512,1024]{1,0:T(8,128)}, f32[512,1024]{1,0:T(8,128)}) fusion(f32[512]{0:T(512)S(1)} %copy-done.3, f32[512,8192]{1,0:T(8,128)} %param.8, f32[8192,1024]{1,0:T(8,128)} %bitcast.59), kind=kOutput, calls=%fused_computation.3 | convolution fusion | flops 51541180416 | bytes 54528000 | tf_op jit(solution)/shard_map/dot_general | solution.py:24
  297.6 2.2 abs.7
  299.8 0.3 reduce_max.9
  300.1 0.2 div.31
  300.3 2.1 div.32
  302.4 1.9 copy.86
  304.4 1.8 copy.88
  306.2 0.0 copy-start.1
  306.2 8.9 %fusion.1 = f32[512,4,2,128]{3,0,2,1:T(8,128)S(1)} fusion(f32[512,4,2,128]{3,0,2,1:T(8,128)} %copy.88, f32[512,4,2,128]{3,2,0,1:T(2,128)} %div.32, f32[512,4]{0,1:T(4,128)S(1)} %mul.46), kind=kLoop, calls=%fused_computation.2 | loop fusion | flops 1048576 | bytes 6299648 | tf_op jit(solution)/shard_map/mul | solution.py:32
  315.1 0.0 copy-done.1
  315.1 2.4 convolution_bitcast_fusion.1
  317.5 1.8 fusion.21
  319.3 0.0 all-reduce.5.cloned.1.call-update
  319.3 0.0 all-reduce.7.cloned.1.call-start
  319.4 83.9 %all-reduce.5.cloned.1.call-done = f32[4,2,64,64]{2,3,1,0:T(8,128)} async-done(((f32[4,2,64,64]{2,3,1,0:T(8,128)}), f32[4,2,64,64]{2,3,1,0:T(8,128)}) %all-reduce.5.cloned.1.call-update) | async-done | bytes 131088 | tf_op jit(solution)/shard_map/psum | solution.py:38
  403.3 1.1 copy.91
  404.3 1.7 fusion.9
  406.0 47.6 %custom-call.8 = f32[4,2,64,64]{3,2,1,0:T(8,128)S(1)} custom-call(f32[4,2,64,64]{3,2,1,0:T(8,128)} %fusion.9), custom_call_target="Cholesky" | custom-call | tf_op jit(solution)/shard_map/jit(cholesky)/cholesky | solution.py:39
  453.7 0.1 compare_reduce_fusion.1
  453.8 0.8 select_bitcast_fusion.1
  454.7 40.0 %custom-call.9 = f32[4,2,1,64,64]{3,4,2,1,0:T(8,128)S(1)} custom-call(f32[4,2,1,64,64]{4,3,2,1,0:T(8,128)} %select_bitcast_fusion.1), custom_call_target="InvertDiagBlocksLowerTriangular" | custom-call | tf_op jit(solution)/shard_map/jit(_solve_triangular)/vmap(vmap())/triangular_solve | solution.py:41
  494.7 0.6 fusion.7
  495.3 1.0 convolution_bitcast_fusion.2
  496.3 2.2 fusion.22
  498.5 0.0 all-reduce.7.cloned.1.call-update
  498.6 0.0 all-reduce.9.cloned.1.call-start
  498.6 83.5 %all-reduce.7.cloned.1.call-done = f32[4,2,128,64]{2,3,1,0:T(8,128)} async-done(((f32[4,2,128,64]{2,3,1,0:T(8,128)}), f32[4,2,128,64]{2,3,1,0:T(8,128)}) %all-reduce.7.cloned.1.call-update) | async-done | bytes 262160 | tf_op jit(solution)/shard_map/psum | solution.py:44
  582.1 3.3 convolution_bitcast_fusion
  585.4 1.8 fusion.23
  587.2 0.0 all-reduce.9.cloned.1.call-update
  587.2 0.0 all-reduce.11.cloned.1.call-start
  587.3 83.6 %all-reduce.9.cloned.1.call-done = f32[4,2,64,64]{2,3,1,0:T(8,128)} async-done(((f32[4,2,64,64]{2,3,1,0:T(8,128)}), f32[4,2,64,64]{2,3,1,0:T(8,128)}) %all-reduce.9.cloned.1.call-update) | async-done | bytes 131088 | tf_op jit(solution)/shard_map/psum | solution.py:38
  670.8 1.1 copy.96
  671.9 1.7 fusion.6
  673.6 47.6 %custom-call.10 = f32[4,2,64,64]{3,2,1,0:T(8,128)S(1)} custom-call(f32[4,2,64,64]{3,2,1,0:T(8,128)} %fusion.6), custom_call_target="Cholesky" | custom-call | tf_op jit(solution)/shard_map/jit(cholesky)/cholesky | solution.py:39
  721.3 0.1 compare_reduce_fusion
  721.4 0.8 select_bitcast_fusion
  722.2 40.0 %custom-call.11 = f32[4,2,1,64,64]{3,4,2,1,0:T(8,128)S(1)} custom-call(f32[4,2,1,64,64]{4,3,2,1,0:T(8,128)} %select_bitcast_fusion), custom_call_target="InvertDiagBlocksLowerTriangular" | custom-call | tf_op jit(solution)/shard_map/jit(_solve_triangular)/vmap(vmap())/triangular_solve | solution.py:41
  762.3 0.6 fusion.4
  762.9 1.8 multiply_convert_fusion
  764.7 0.0 copy-start
  764.7 2.2 fusion.2
  766.9 0.0 all-reduce.11.cloned.1.call-update
  766.9 0.0 copy-done
  766.9 1.0 copy.100
  767.9 82.5 %all-reduce.11.cloned.1.call-done = f32[4,2,128,64]{2,3,1,0:T(8,128)} async-done(((f32[4,2,128,64]{2,3,1,0:T(8,128)}), f32[4,2,128,64]{2,3,1,0:T(8,128)}) %all-reduce.11.cloned.1.call-update) | async-done | bytes 262160 | tf_op jit(solution)/shard_map/psum | solution.py:44
  850.5 1.0 broadcast_multiply_fusion
  851.4 0.8 copy.101
  (7 shorter events, 0.1 us)
Async XLA Ops:
  7.2 0.8 copy-start.2
  7.2 202.4 %all-gather.2.cloned.1.call-start = ((), (), s32[]{:S(2)}) async-start(), calls=%async_computation | async-start | bytes 35651584 | tf_op jit(solution)/shard_map/all_gather | solution.py:22
  7.9 395.4 %all-reduce.5.cloned.1.call-start = ((), (), s32[]{:S(2)}) async-start(), calls=%async_computation.1 | async-start | bytes 524288 | tf_op jit(solution)/shard_map/psum | solution.py:38
  209.6 27.5 %copy-start.3 = (f32[512]{0:T(512)S(1)}, f32[512]{0:T(512)}, u32[]{:S(2)}) copy-start(f32[512]{0:T(512)} %param.9) | copy-start | bytes 6148
  306.2 8.9 %copy-start.1 = (s32[4,2,128,64]{2,3,1,0:T(8,128)S(1)}, s32[4,2,128,64]{2,3,1,0:T(8,128)}, u32[]{:S(2)}) copy-start(s32[4,2,128,64]{2,3,1,0:T(8,128)} %param.12) | copy-start | bytes 786436
  319.3 262.8 %all-reduce.7.cloned.1.call-start = ((), (), s32[]{:S(2)}) async-start(), calls=%async_computation.2 | async-start | bytes 524288 | tf_op jit(solution)/shard_map/psum | solution.py:44
  498.6 172.3 %all-reduce.9.cloned.1.call-start = ((), (), s32[]{:S(2)}) async-start(), calls=%async_computation.3 | async-start | bytes 524288 | tf_op jit(solution)/shard_map/psum | solution.py:38
  587.2 263.2 %all-reduce.11.cloned.1.call-start = ((), (), s32[]{:S(2)}) async-start(), calls=%async_computation.4 | async-start | bytes 524288 | tf_op jit(solution)/shard_map/psum | solution.py:44
  764.7 2.3 copy-start
Sparse Core Ops, SparseCore 0:
  10.1 199.3 all-gather.1
  319.4 83.7 all-reduce.4
  498.7 83.3 all-reduce.6
  587.3 83.4 all-reduce.8
  767.1 83.3 all-reduce.10
where the time goes:
time: 860 us; the launch traced here: 859 us
  waiting for transfers between devices  536 us (62%)
  other arithmetic  191 us (22%)
  matrix products  78.2 us (9%)
  local copies, waits for them, and re-layouts  39.9 us (5%)
  between operations  14 us (2%)
    all_gather x1, waiting for transfers between devices, shards(): weight_piece = lax.all_gather(key_value_weight, 'seq', axis=0, tiled=True)  201 us
    psum x2, waiting for transfers between devices, shards(): gram_matrix = lax.psum(local_gram, 'seq')  167 us
    psum x2, waiting for transfers between devices, shards(): coefficient_rows = lax.psum(local_coef, 'seq')  166 us
    another operation x7, other arithmetic, shards(): lower_factor = jnp.linalg.cholesky(gram_matrix)  95.6 us
    another operation x5, other arithmetic, shards(): jax.scipy.linalg.solve_triangular(lower_factor, identity, lower=True)  81.7 us
    dot_general x1, matrix products, shards(): projected_key_value = jnp.dot(hidden, flat_piece, precision=highest)  60.5 us
    unnamed x11, local copies, waits for them, and re-layouts  29.4 us
  transfers between devices with their start and end apart: 5, of which 5 were waited for; matrix products, arithmetic and copies ran while one was open for 0% of the time, Pallas kernels for 0%

commit v1 on v0

v1 whole, which is shorter than its diff:
```python
import functools
import math

import jax
import jax.numpy as jnp
from jax import lax
from jax.experimental import pallas as pl
from jax.experimental.pallas import tpu as pltpu
from jax.sharding import PartitionSpec as P

GROUP = 64
RANK = 64
F32 = jnp.float32
BF16 = jnp.bfloat16
HIGHEST = lax.Precision.HIGHEST

SINE = [(-1) ** n * (2.0 * math.pi) ** (2 * n + 1) / math.factorial(2 * n + 1) for n in range(7)]


def split(x):
    high = x.astype(BF16)
    low = (x - high.astype(F32)).astype(BF16)
    return high, low


def sine_of_cycles(u):
    r = u - jnp.floor(u + 0.5)
    r = jnp.where(r > 0.25, 0.5 - r, jnp.where(r < -0.25, -0.5 - r, r))
    t = r * r
    p = jnp.full_like(t, SINE[-1])
    for c in SINE[-2::-1]:
        p = p * t + c
    return r * p


def dot(a, b, contract):
    return lax.dot_general(
        a, b, ((contract[:1], contract[1:]), ((), ())), precision=HIGHEST, preferred_element_type=F32
    )


def three_products(x, w):
    xh, xl = split(x)
    wh, wl = split(w)
    return jnp.dot(
        jnp.concatenate([xh, xl, xh], axis=1),
        jnp.concatenate([wh, wh, wl], axis=0),
        preferred_element_type=F32,
    )


def residual(kv, keep):
    tokens, cols = kv.shape
    grouped = kv.reshape(tokens // GROUP, GROUP, cols)
    step = jnp.max(jnp.abs(grouped), axis=1, keepdims=True) / 7.0 + 1e-06
    s = sine_of_cycles(grouped * (1.0 / step)) * keep[:, None, :]
    return s.reshape(tokens, cols)


def project_kernel(hidden_ref, weight_ref, scale_ref, keep_ref, high_ref, low_ref, gram_ref, acc_ref):
    k = pl.program_id(0)

    @pl.when(k == 0)
    def _():
        acc_ref[...] = jnp.zeros_like(acc_ref)

    rows = weight_ref.shape[0] * weight_ref.shape[2]
    acc_ref[...] += three_products(hidden_ref[...], weight_ref[...].reshape(rows, weight_ref.shape[3]))

    @pl.when(k == pl.num_programs(0) - 1)
    def _():
        for p in range(acc_ref.shape[1] // 128):
            cols = slice(128 * p, 128 * p + 128)
            kv = acc_ref[:, cols] * scale_ref[...]
            r = residual(kv, keep_ref[:, cols])
            rh, rl = split(r)
            high_ref[:, cols] = rh
            low_ref[:, cols] = rl
            gram_ref[128 * p : 128 * p + 128, :] = lax.dot_general(
                jnp.concatenate([rh, rh, rl], axis=0),
                jnp.concatenate([rh, rl, rh], axis=0),
                (((0,), (0,)), ((), ())),
                preferred_element_type=F32,
            )


def inverse_factors(grams):
    n = len(grams)
    lane = lax.broadcasted_iota(jnp.int32, (RANK, 128), 1)
    row = lax.broadcasted_iota(jnp.int32, (RANK, 128), 0)
    unit = jnp.where(lane - RANK == row, 1.0, 0.0).astype(F32)
    full = jnp.stack([jnp.where(lane < RANK, g, unit) for g in grams])
    blocks = [full[:, 8 * i : 8 * i + 8, :] for i in range(RANK // 8)]
    sub = lax.broadcasted_iota(jnp.int32, (n, 8, 1), 1)
    for j in range(RANK):
        jb, js = divmod(j, 8)
        pivot_row = blocks[jb][:, js : js + 1, :]
        scaled = pivot_row * (1.0 / pivot_row[:, :, j : j + 1])
        for i in range(jb, RANK // 8):
            column = blocks[i][:, :, j : j + 1]
            if i == jb:
                column = jnp.where(sub > js, column, 0.0)
            blocks[i] = blocks[i] - column * scaled
    full = jnp.concatenate(blocks, axis=1)
    out = []
    for p in range(n):
        a = full[p]
        pivots = jnp.sum(jnp.where(lane == row, a, 0.0), axis=1, keepdims=True)
        out.append(jnp.where(lane < RANK, 0.0, a) * lax.rsqrt(pivots))
    return out


def basis_start_kernel(sign_ref, out_ref):
    pairs = sign_ref.shape[0]
    inverses = inverse_factors([dot(sign_ref[p], sign_ref[p], (0, 0))[:RANK] for p in range(pairs)])
    for p in range(pairs):
        out_ref[p] = dot(sign_ref[p], jnp.concatenate([inverses[p]] * 2, axis=0), (1, 1))


def factor_kernel(root_length, gram_ref, start_ref, high_ref, low_ref, left_ref, right_ref):
    pairs = start_ref.shape[0]
    eye = lax.broadcasted_iota(jnp.int32, (128, 128), 0) == lax.broadcasted_iota(jnp.int32, (128, 128), 1)
    scales, ys, zs, grams = [], [], [], []
    for p in range(pairs):
        g = gram_ref[128 * p : 128 * p + 128, :]
        size = jnp.sum(jnp.sum(jnp.where(eye, g, 0.0), axis=1, keepdims=True), axis=0, keepdims=True) / 128.0
        g = g * (1.0 / size)
        y = dot(g, start_ref[p], (1, 0))
        z = dot(g, y, (1, 0))
        scales.append(size)
        ys.append(y)
        zs.append(z)
        grams.append(dot(y, z, (0, 0))[:RANK])
    inverses = inverse_factors(grams)
    zero = jnp.zeros((RANK, 128), F32)
    for h in range(pairs // 2):
        tops, rights = [], None
        for e in range(2):
            p = 2 * h + e
            wide = jnp.concatenate([inverses[p], zero] if e == 0 else [zero, inverses[p]], axis=0)
            tops.append(dot(ys[p], wide, (1, 1)) * (lax.rsqrt(scales[p]) * root_length))
            part = dot(zs[p], wide, (1, 1)) * (jnp.sqrt(scales[p]) * (1.0 / root_length))
            rights = part if rights is None else rights + part
        right_ref[h] = rights
        th, tl = split(jnp.concatenate(tops, axis=0))
        cols = slice(256 * h, 256 * h + 256)
        rh = high_ref[:, cols]
        rl = low_ref[:, cols]
        left_ref[h] = jnp.dot(
            jnp.concatenate([rh, rl, rh], axis=1),
            jnp.concatenate([th, th, tl], axis=0),
            preferred_element_type=F32,
        ).astype(BF16)


def shards(hidden, row_scale, key_value_weight, outlier, sketch_sign_flags):
    tokens, width = hidden.shape
    rows, heads, kv_cols = key_value_weight.shape
    cols = heads * kv_cols
    pairs = 2 * heads
    groups = outlier.shape[0]
    seq = lax.axis_size("seq")
    batch = lax.axis_size("batch")
    quarter = rows // batch
    root_length = math.sqrt(tokens * seq)

    own = lax.dynamic_slice_in_dim(key_value_weight, lax.axis_index("batch") * quarter, quarter, 0)
    weight = lax.all_gather(own.reshape(quarter, cols), ("batch", "seq"), axis=0)
    weight = weight.reshape(batch, seq, quarter, cols)

    signs = (2 * sketch_sign_flags - 1).astype(F32).reshape(pairs, 128, RANK)
    start = pl.pallas_call(
        basis_start_kernel,
        out_shape=jax.ShapeDtypeStruct((pairs, 128, 128), F32),
        name="start",
        cost_estimate=pl.CostEstimate(flops=10**8, bytes_accessed=10**6, transcendentals=0),
    )(jnp.concatenate([signs, signs], axis=2))

    keep = jnp.repeat((1 - outlier).astype(F32), kv_cols, axis=1)
    whole = lambda *shape: pl.BlockSpec(shape, lambda k: (0,) * len(shape))
    high, low, gram = pl.pallas_call(
        project_kernel,
        grid=(seq,),
        in_specs=[
            pl.BlockSpec((tokens, rows), lambda k: (0, k)),
            pl.BlockSpec((batch, 1, quarter, cols), lambda k: (0, k, 0, 0)),
            whole(tokens, 1),
            whole(groups, cols),
        ],
        out_specs=[whole(tokens, cols), whole(tokens, cols), whole(128 * pairs, 128)],
        out_shape=[
            jax.ShapeDtypeStruct((tokens, cols), BF16),
            jax.ShapeDtypeStruct((tokens, cols), BF16),
            jax.ShapeDtypeStruct((128 * pairs, 128), F32),
        ],
        scratch_shapes=[pltpu.VMEM((tokens, cols), F32)],
        compiler_params=pltpu.CompilerParams(vmem_limit_bytes=40 << 20, dimension_semantics=("arbitrary",)),
        name="project",
        cost_estimate=pl.CostEstimate(flops=6 * tokens * width * cols, bytes_accessed=50 << 20, transcendentals=0),
    )(hidden, weight, row_scale[:, None], keep)

    pieces = lax.all_to_all(gram, "seq", 0, 0, tiled=True)
    piece = jnp.sum(pieces.reshape(seq, 128 * pairs // seq, 128), axis=0)
    gram = lax.all_gather(piece, "seq", axis=0, tiled=True)

    return pl.pallas_call(
        functools.partial(factor_kernel, root_length),
        out_shape=[
            jax.ShapeDtypeStruct((heads, tokens, 2 * RANK), BF16),
            jax.ShapeDtypeStruct((heads, 128, 2 * RANK), F32),
        ],
        compiler_params=pltpu.CompilerParams(vmem_limit_bytes=40 << 20),
        name="factor",
        cost_estimate=pl.CostEstimate(flops=10**9, bytes_accessed=4 << 20, transcendentals=0),
    )(gram, start, high, low)


def solution(mesh):
    return jax.shard_map(
        shards,
        mesh=mesh,
        in_specs=(
            P(("batch", "seq"), None),
            P(("batch", "seq")),
            P("seq", "head", None),
            P(("batch", "seq"), "head"),
            P("head", None, None, None),
        ),
        out_specs=(P("head", ("batch", "seq"), None), P(("batch", "head"), None, None)),
        check_vma=False,
    )
```

time: 860 us -> 282 us (0.33)
  waiting for transfers between devices: 536 us -> 163 us
  other arithmetic: 191 us -> 4.95 us
  matrix products: 78.2 us -> 0 us
  Pallas kernels: 0 us -> 59.7 us
  local copies, waits for them, and re-layouts: 39.9 us -> 7.77 us
  blocking collectives: 0 us -> 24.5 us
    psum x4 -> x0, waiting for transfers between devices: 333 us -> none  [the longest x2 167 us: shards(): gram_matrix = lax.psum(local_gram, 'seq')]
    another operation x12 -> x0, other arithmetic: 177 us -> none  [the longest x7 95.6 us: shards(): lower_factor = jnp.linalg.cholesky(gram_matrix)]
    dot_general x9 -> x0, matrix products: 77 us -> none  [the longest x1 60.5 us: shards(): projected_key_value = jnp.dot(hidden, flat_piece, precision=highest)]
    pallas_call x0 -> x3, Pallas kernels: none -> 59.7 us  [the longest x1 36.3 us: shards(): pl.pallas_call(project_kernel, grid=(seq,), in_specs=[pl.BlockSpec((token...]
    all_gather x1, waiting for transfers between devices: 201 us -> 163 us  [shards(): lax.all_gather(own.reshape(quarter, cols), ('batch', 'seq'), axis=0)]
    unnamed x11 -> x8, local copies, waits for them, and re-layouts: 29.4 us -> 4.77 us
    all_gather x0 -> x1, blocking collectives: none -> 24.5 us  [shards(): gram = lax.all_gather(piece, 'seq', axis=0, tiled=True)]
    mul x1 -> x0, other arithmetic: 8.89 us -> none  [shards(): retain_mask * jnp.sin(complete_cycle * grouped_rows / quantization_spacing)]
  transfers between devices with their start and end apart: 5 -> 2, of which waited for: 5 -> 1; matrix products, arithmetic and copies ran while one was open for 0% -> 2% of each run, Pallas kernels for 0% -> 4%
where the time goes in v1:
time: 282 us; the launch traced here: 281 us
  waiting for transfers between devices  163 us (58%)
  Pallas kernels  59.7 us (21%)
  blocking collectives  24.5 us (9%)
  between operations  14.1 us (5%)
  local copies, waits for them, and re-layouts  7.77 us (3%)
  starting transfers between devices  6.89 us (2%)
  other arithmetic  4.95 us (2%)
    all_gather x1, waiting for transfers between devices, shards(): lax.all_gather(own.reshape(quarter, cols), ('batch', 'seq'), axis=0)  163 us
    pallas_call x1, Pallas kernels, shards(): pl.pallas_call(project_kernel, grid=(seq,), in_specs=[pl.BlockSpec((token...  36.3 us
    all_gather x1, blocking collectives, shards(): gram = lax.all_gather(piece, 'seq', axis=0, tiled=True)  24.5 us
    pallas_call x1, Pallas kernels, shards(): pl.pallas_call(functools.partial(factor_kernel, root_length), out_shape=[...  12.2 us
    pallas_call x1, Pallas kernels, shards(): pl.pallas_call(basis_start_kernel, out_shape=jax.ShapeDtypeStruct((pairs,...  11.2 us
    all_to_all x1, starting transfers between devices, shards(): pieces = lax.all_to_all(gram, 'seq', 0, 0, tiled=True)  6.86 us
  transfers between devices with their start and end apart: 2, of which 1 were waited for; matrix products, arithmetic and copies ran while one was open for 2% of the time, Pallas kernels for 4%

profile of v1, /device:TPU:0, one launch (start us, length us, event | category | flops | bytes accessed | tf_op | source)
XLA Modules:
  0.0 281.3 jit_solution(12760943502861897901)
XLA Ops:
  7.2 0.0 copy-start
  7.2 0.0 all-gather.2.cloned.1.call-start
  7.2 1.5 copy-done
  8.8 1.1 all_gather_reshape.3
  9.9 0.0 all-gather.2.cloned.1.call-update
  9.9 0.8 copy.10.scale_ref
  10.7 0.7 subtract_convert_fusion
  11.4 163.4 %all-gather.2.cloned.1.call-done = f32[64,128,1024]{2,1,0:T(8,128)} async-done(((f32[1,128,1024]{2,1,0:T(8,128)}), f32[64,128,1024]{2,1,0:T(8,128)}) %all-gather.2.cloned.1.call-update) | async-done | bytes 33554448 | tf_op jit(solution)/shard_map/all_gather | solution.py:168
  174.8 0.1 broadcast_in_dim.7
  174.9 36.3 %project.1 = (bf16[512,1024]{1,0:T(8,128)(2,1)S(1)}, bf16[512,1024]{1,0:T(8,128)(2,1)S(1)}, f32[1024,128]{1,0:T(8,128)}) custom-call(f32[512,8192]{1,0:T(8,128)} %hidden_ref.1, f32[4,16,128,1024]{3,2,1,0:T(8,128)} %bitcast.8, f32[512,1]{1,0:T(8,128)S(1)} %copy.10.scale_ref, f32[8,1024]{1,0:T(8,128)S(1)} %bitcast.5), custom_call_target="tpu_custom_call" | custom-call | flops 25769803776 | bytes 52428800 | tf_op jit(solution)/shard_map/project/pallas_call | solution.py:181
  211.1 0.0 copy-start.2
  211.1 1.0 copy-done.2
  212.1 6.9 %all-to-all-start = ((f32[16,64,128]{2,1,0:T(8,128)}), f32[16,64,128]{2,1,0:T(8,128)}, u32[]{:S(2)}, u32[]{:S(2)}) async-start(f32[16,64,128]{2,1,0:T(8,128)} %bitcast.3), calls=%async_computation | async-start | bytes 1048576 | tf_op jit(solution)/shard_map/all_to_all | solution.py:202
  218.9 1.0 add_convert_fusion
  219.9 1.0 copy.11
  220.9 2.2 pad_maximum_fusion.sign_ref
  223.1 11.2 %start.1.start_ref = f32[8,128,128]{2,1,0:T(8,128)} custom-call(f32[8,128,128]{2,1,0:T(8,128)} %pad_maximum_fusion.sign_ref), custom_call_target="tpu_custom_call" | custom-call | flops 100000000 | bytes 1000000 | tf_op jit(solution)/shard_map/start/pallas_call | solution.py:172
  234.3 0.0 all-to-all-done
  234.3 1.1 reduce_sum.9
  235.4 24.5 %all_gather.7.gram_ref = f32[1024,128]{1,0:T(8,128)S(1)} all-gather(f32[64,128]{1,0:T(8,128)S(1)} %reduce_sum.9), channel_id=1, replica_groups=mesh['batch'=4,'head'=2,'seq'=16] {'seq'}, dimensions={0}, use_global_device_ids=true | all-gather | bytes 557056 | tf_op jit(solution)/shard_map/all_gather | solution.py:204
  260.0 0.0 copy-start.1
  260.0 1.0 copy-done.1
  261.0 0.0 copy-start.3
  261.0 1.2 copy-done.3
  262.2 12.2 %factor.1 = (bf16[4,512,128]{2,1,0:T(8,128)(2,1)}, f32[4,128,128]{2,1,0:T(8,128)}) custom-call(f32[1024,128]{1,0:T(8,128)S(1)} %all_gather.7.gram_ref, f32[8,128,128]{2,1,0:T(8,128)S(1)} %copy-done.1, bf16[512,1024]{1,0:T(8,128)(2,1)S(1)} %get-tuple-element.6.high_ref, bf16[512,1024]{1,0:T(8,128)(2,1)S(1)} %copy-done.3), custom_call_target="tpu_custom_call" | custom-call | flops 1000000000 | bytes 4194304 | tf_op jit(solution)/shard_map/factor/pallas_call | solution.py:206
  (1 shorter events, 0.0 us)
Async XLA Ops:
  7.2 1.6 copy-start
  7.2 167.6 %all-gather.2.cloned.1.call-start = ((), (), s32[]{:S(2)}) async-start(), calls=%async_computation.1 | async-start | bytes 34078720 | tf_op jit(solution)/shard_map/all_gather | solution.py:168
  211.1 1.0 copy-start.2
  212.1 22.3 %all-to-all-start = ((f32[16,64,128]{2,1,0:T(8,128)}), f32[16,64,128]{2,1,0:T(8,128)}, u32[]{:S(2)}, u32[]{:S(2)}) async-start(f32[16,64,128]{2,1,0:T(8,128)} %bitcast.3), calls=%async_computation | async-start | bytes 1048576 | tf_op jit(solution)/shard_map/all_to_all | solution.py:202
  260.0 1.0 copy-start.1
  261.0 1.2 copy-start.3
Sparse Core Ops, SparseCore 0:
  11.5 163.2 all-gather.1
